TPU v7x, 512 devices: a whole 4x4x16 slice. The times are simulated.
512 devices in a mesh: space: 32 (over z, core), tm: 16 (over y, x).
Axes of the slice: x: 4, y: 4, z: 16, core: 2. Of those that a mesh axis runs over, the one named last changes fastest.
Arguments:
- snapshots: bfloat16 [65536, 16384], P('space', 'tm'), may hold values from -6 to 6
- basis: bfloat16 [65536, 256], P(('space', 'tm')), may hold values from -0.0234375 to 0.0234375
- lengths: int32 [16, 64], P('tm'), may hold values from 1 to 61, as said below
- owners: int32 [16, 64], P('tm'), may hold values from 0 to 31, as said below
Outputs:
- gram_out: bfloat16 [16, 32, 392, 392], P('tm', 'space')
- target_out: bfloat16 [16, 32, 392, 256], P('tm', 'space')
Inputs may be any that keep to these rules, and one draw needn't show every extreme that they name: Each row of lengths sums to 1024. The trajectories that one owner holds in one row have 62 snapshots together at most, and in every row some owner holds exactly 62. `owners`: in every row each space index owns exactly two trajectories.
All inputs are finite; a program needn't handle non-finite values.
Results may differ from a plain program's by a relative error of at most 0.0057.
Values may be sent and summed in bfloat16 or wider, within the bound.
No kernel may reach another device: no remote copies, remote signals or barrier semaphores. Data moves between devices by JAX's collectives and lax.ppermute only.
A program may use at most 64 MiB of HBM per device.

v0:
```python
import jax
import jax.numpy as jnp
import numpy as np
from jax import lax
from jax.sharding import PartitionSpec as P

QM = 16


def slot_plan(length_row, owner_row, owner_count, capacity, snap_count):
    traj_end = jnp.cumsum(length_row)
    starts = traj_end - length_row
    snap_index = jnp.arange(snap_count, dtype=jnp.int32)
    member = (
        (snap_index[:, None] >= starts[None, :]) & (snap_index[:, None] < traj_end[None, :])
    ).astype(jnp.int32)
    snap_start = jnp.sum(member * starts[None, :], axis=1)
    snap_end = jnp.sum(member * traj_end[None, :], axis=1)
    snap_owner = jnp.sum(member * owner_row[None, :], axis=1)
    traj_index = jnp.arange(length_row.shape[0], dtype=jnp.int32)
    same_owner = owner_row[:, None] == owner_row[None, :]
    earlier = traj_index[None, :] < traj_index[:, None]
    offset = jnp.sum(jnp.where(same_owner & earlier, length_row[None, :], 0), axis=1)
    slot_index = jnp.sum(member * offset[None, :], axis=1) + snap_index - snap_start
    has_next = (snap_index + 1 < snap_end).astype(jnp.int32)
    destination = snap_owner * capacity + slot_index
    source_rows = jnp.full((owner_count * capacity,), -1, jnp.int32).at[destination].set(snap_index)
    live_rows = jnp.zeros((owner_count * capacity,), jnp.int32).at[destination].set(has_next)
    return (source_rows, live_rows)


def library(coords, live_slots, weight_scale):
    first_mode, second_mode = np.triu_indices(QM)
    products = coords[:, first_mode] * coords[:, second_mode]
    library_rows = jnp.concatenate([coords, products], axis=1).astype(jnp.bfloat16)
    successor = jnp.concatenate(
        [coords[1:], jnp.zeros((1, coords.shape[1]), jnp.float32)], axis=0
    ).astype(jnp.bfloat16)
    weighted = library_rows * live_slots[:, None].astype(jnp.bfloat16)
    dims = (((0,), (0,)), ((), ()))
    gram_matrix = (
        lax.dot_general(weighted, library_rows, dims, preferred_element_type=jnp.float32)
        * weight_scale
    )
    targets = (
        lax.dot_general(weighted, successor, dims, preferred_element_type=jnp.float32)
        * weight_scale
    )
    return (gram_matrix.astype(jnp.bfloat16), targets.astype(jnp.bfloat16))


def on_device(snapshots, basis, lengths, owners):
    dims = (((0,), (0,)), ((), ()))
    snap_count = snapshots.shape[1]
    gathered = lax.all_gather(basis, "tm", axis=0, tiled=True)
    partial_value = lax.dot_general(snapshots, gathered, dims, preferred_element_type=jnp.float32)
    owner_count = lax.axis_size("space")
    capacity = 2 * snap_count // owner_count - 2
    source_rows, live_rows = slot_plan(lengths[0], owners[0], owner_count, capacity, snap_count)
    own_index = lax.axis_index("space")
    mine = lax.dynamic_slice_in_dim(source_rows, own_index * capacity, capacity)
    summed = lax.psum(partial_value, "space")
    packed = jnp.take(summed, jnp.maximum(mine, 0), axis=0) * (mine >= 0)[:, None].astype(
        jnp.float32
    )
    live_slots = lax.dynamic_slice_in_dim(live_rows, own_index * capacity, capacity)
    gram_matrix, targets = library(packed, live_slots, owner_count / snap_count)
    return (gram_matrix[None, None], targets[None, None])


def solution(mesh):
    placed = (P("space", "tm"), P(("space", "tm"), None), P("tm", None), P("tm", None))
    return jax.shard_map(
        on_device,
        mesh=mesh,
        in_specs=placed,
        out_specs=(P("tm", "space", None, None), P("tm", "space", None, None)),
        check_vma=False,
    )
```

profile of v0, /device:TPU:1, one launch (start us, length us, event | category | flops | bytes accessed | tf_op | source)
XLA Modules:
  0.0 301.7 jit_solution(7914927873324652971)
XLA Ops:
  7.2 0.0 all-gather.2.cloned.1.call-start
  7.2 0.7 all-gather.2.cloned.1.call-update
  7.9 0.0 all-reduce.3.cloned.1.call-start
  7.9 0.7 copy.20
  8.7 0.1 reduce-window.4
  8.8 0.1 reduce
  8.9 0.9 select_reduce_fusion.4
  9.8 0.7 fusion.17
  10.5 0.8 select_reduce_fusion
  11.4 4.3 %scatter_custom_fusion.1 = s32[1984]{0:T(1024)S(1)} fusion(s32[1024]{0:T(1024)S(1)} %bitcast.28, s32[1024]{0:T(1024)S(1)} %fusion.16, s32[]{:T(128)} %constant.22.clone.1), kind=kCustom, calls=%fused_computation.35 | custom fusion | bytes 7940 | tf_op jit(solution)/shard_map/scatter | solution.py:28
  15.7 4.3 %scatter_custom_fusion = s32[1984]{0:T(1024)S(1)} fusion(s32[1024]{0:T(1024)S(1)} %bitcast.29, s32[1024]{0:T(1024)S(1)} %iota.19, s32[]{:T(128)} %constant.21.clone.1), kind=kCustom, calls=%fused_computation.37 | custom fusion | bytes 7940 | tf_op jit(solution)/shard_map/scatter | solution.py:27
  20.0 0.0 copy-start.1
  20.1 0.0 copy-start
  20.1 52.9 %all-gather.2.cloned.1.call-done = bf16[2048,256]{1,0:T(8,128)(2,1)} async-done(((bf16[128,256]{1,0:T(8,128)(2,1)}), bf16[2048,256]{1,0:T(8,128)(2,1)}) %all-gather.2.cloned.1.call-update) | async-done | bytes 1048592 | tf_op jit(solution)/shard_map/all_gather | solution.py:55
  72.9 4.8 %fusion.22 = f32[1024,256]{1,0:T(8,128)} fusion(bf16[2048,1024]{1,0:T(8,128)(2,1)} %param.8, bf16[2048,256]{1,0:T(8,128)(2,1)} %all-gather.2.cloned.1.call-done), kind=kOutput, calls=%fused_computation.51 | convolution fusion | flops 1073741824 | bytes 6291456 | tf_op jit(solution)/shard_map/dot_general | solution.py:56
  77.7 0.0 all-reduce.3.cloned.1.call-update
  77.7 0.1 dynamic-slice_convert_fusion
  77.8 0.1 broadcast_compare_fusion
  77.9 0.0 copy-done.1
  77.9 0.0 copy-done
  77.9 211.2 %all-reduce.3.cloned.1.call-done = f32[1024,256]{1,0:T(8,128)} async-done(((f32[1024,256]{1,0:T(8,128)}), f32[1024,256]{1,0:T(8,128)}) %all-reduce.3.cloned.1.call-update) | async-done | bytes 1048592 | tf_op jit(solution)/shard_map/psum | solution.py:62
  289.2 1.9 gather_fusion
  291.0 0.1 fusion.21
  291.1 0.1 copy.21
  291.2 0.7 gather_fusion.2
  291.9 0.7 gather_fusion.1
  292.6 0.1 copy.23
  292.7 0.1 copy.24
  292.8 1.1 fusion.1
  293.9 1.0 fusion.3
  (9 shorter events, 0.1 us)
Async XLA Ops:
  7.2 65.8 %all-gather.2.cloned.1.call-start = ((), (), s32[]{:S(2)}) async-start(), calls=%async_computation | async-start | bytes 1114112 | tf_op jit(solution)/shard_map/all_gather | solution.py:55
  7.9 281.3 %all-reduce.3.cloned.1.call-start = ((), (), s32[]{:S(2)}) async-start(), calls=%async_computation.1 | async-start | bytes 2097152 | tf_op jit(solution)/shard_map/psum | solution.py:62
  20.0 57.8 %copy-start.1 = (s32[136]{0:T(256)S(1)}, s32[136]{0:T(256)}, u32[]{:S(2)}) copy-start(s32[136]{0:T(256)} %constant.68) | copy-start | bytes 1636
  20.1 57.8 %copy-start = (s32[136]{0:T(256)S(1)}, s32[136]{0:T(256)}, u32[]{:S(2)}) copy-start(s32[136]{0:T(256)} %constant.69) | copy-start | bytes 1636
Sparse Core Ops, SparseCore 0:
  11.0 61.8 all-gather.1
  77.8 211.2 all-reduce.2
where the time goes:
time: 302 us
  waiting for transfers between devices  265 us (88%)
  between operations  14.2 us (5%)
  local copies, waits for them, and re-layouts  12.9 us (4%)
  matrix products  6.86 us (2%)
    psum x1, waiting for transfers between devices, on_device(): summed = lax.psum(partial_value, 'space')  211 us
    all_gather x1, waiting for transfers between devices, on_device(): gathered = lax.all_gather(basis, 'tm', axis=0, tiled=True)  52.9 us
  transfers between devices with their start and end apart: 2, of which 2 were waited for; matrix products, arithmetic and copies ran while one was open for 4% of the time, Pallas kernels for 0%

commit v1 on v0

--- a/solution.py
+++ b/solution.py
@@ -5,6 +5,32 @@
 from jax.sharding import PartitionSpec as P
 
 QM = 16
+
+
+def cut_the_words(arr_in, which_dim):
+    group_axis = "tm"
+    local_part = jax.lax.axis_size(group_axis)
+    f_now = jax.lax.axis_index(group_axis)
+    res, extra, s_next = (local_part, f_now, arr_in.shape[which_dim])
+    rows = [(d, (d + 1) % res) for d in range(res)]
+    tray = [(d, (d - 1) % res) for d in range(res)]
+    parts_out = jnp.zeros(
+        (*arr_in.shape[:which_dim], res * s_next, *arr_in.shape[which_dim + 1 :]), arr_in.dtype
+    )
+    parts_out = lax.dynamic_update_slice_in_dim(parts_out, arr_in, extra * s_next, axis=which_dim)
+    tmp = r1 = arr_in
+    val = res // 2
+    for t in tuple(range(1, val + 1)):
+        tmp = jax.lax.ppermute(tmp, group_axis, rows)
+        parts_out = lax.dynamic_update_slice_in_dim(
+            parts_out, tmp, (extra - t) % res * s_next, axis=which_dim
+        )
+        if t < res - val:
+            r1 = jax.lax.ppermute(r1, group_axis, tray)
+            parts_out = lax.dynamic_update_slice_in_dim(
+                parts_out, r1, (extra + t) % res * s_next, axis=which_dim
+            )
+    return parts_out
 
 
 def slot_plan(length_row, owner_row, owner_count, capacity, snap_count):
@@ -52,7 +78,7 @@
 def on_device(snapshots, basis, lengths, owners):
     dims = (((0,), (0,)), ((), ()))
     snap_count = snapshots.shape[1]
-    gathered = lax.all_gather(basis, "tm", axis=0, tiled=True)
+    gathered = cut_the_words(basis, 0)
     partial_value = lax.dot_general(snapshots, gathered, dims, preferred_element_type=jnp.float32)
     owner_count = lax.axis_size("space")
     capacity = 2 * snap_count // owner_count - 2

time: 302 us -> 325 us (1.076)
  starting transfers between devices: 0.08 us -> 63.4 us
  waiting for transfers between devices: 265 us -> 222 us
    ppermute x0 -> x15, starting transfers between devices: none -> 63.4 us  [the longest x7 46 us: cut_the_words(): r1 = jax.lax.ppermute(r1, group_axis, tray)]
    all_gather x1 -> x0, waiting for transfers between devices: 52.9 us -> none  [on_device(): gathered = lax.all_gather(basis, 'tm', axis=0, tiled=True)]
    ppermute x0 -> x15, waiting for transfers between devices: none -> 6.66 us  [the longest x8 6.64 us: cut_the_words(): tmp = jax.lax.ppermute(tmp, group_axis, rows)]
    psum x1, waiting for transfers between devices: 211 us -> 216 us  [on_device(): summed = lax.psum(partial_value, 'space')]
  transfers between devices with their start and end apart: 2 -> 16, of which waited for: 2 -> 3; matrix products, arithmetic and copies ran while one was open for 4% -> 4% of each run, Pallas kernels for 0% -> 0%
where the time goes in v1:
time: 325 us; the launch traced here: 324 us
  waiting for transfers between devices  222 us (68%)
  starting transfers between devices  63.4 us (20%)
  between operations  14.9 us (5%)
  local copies, waits for them, and re-layouts  14.3 us (4%)
  matrix products  6.61 us (2%)
    psum x1, waiting for transfers between devices, on_device(): summed = lax.psum(partial_value, 'space')  216 us
    ppermute x7, starting transfers between devices, cut_the_words(): r1 = jax.lax.ppermute(r1, group_axis, tray)  46 us
    ppermute x8, starting transfers between devices, cut_the_words(): tmp = jax.lax.ppermute(tmp, group_axis, rows)  17.4 us
    ppermute x8, waiting for transfers between devices, cut_the_words(): tmp = jax.lax.ppermute(tmp, group_axis, rows)  6.64 us
  transfers between devices with their start and end apart: 16, of which 3 were waited for; matrix products, arithmetic and copies ran while one was open for 4% of the time, Pallas kernels for 0%

profile of v1, /device:TPU:1, one launch (start us, length us, event | category | flops | bytes accessed | tf_op | source)
XLA Modules:
  0.0 324.4 jit_solution(5802631841943797560)
XLA Ops:
  7.2 0.0 all-reduce.3.cloned.1.call-start
  7.2 4.0 %collective-permute-start = (bf16[128,256]{1,0:T(8,128)(2,1)}, bf16[128,256]{1,0:T(8,128)(2,1)S(1)}, u32[]{:S(2)}, u32[]{:S(2)}) collective-permute-start(bf16[128,256]{1,0:T(8,128)(2,1)} %param.9), channel_id=1, source_target_pairs={{0,1},{1,2},{2,3},{3,4},{4,5},{5,6},{6,7},{7,8},{8,9},{9,10},{10,1... | collective-permute-start | bytes 196616 | tf_op jit(solution)/shard_map/ppermute | solution.py:24
  11.2 5.6 %collective-permute-start.1 = (bf16[128,256]{1,0:T(8,128)(2,1)}, bf16[128,256]{1,0:T(8,128)(2,1)S(1)}, u32[]{:S(2)}, u32[]{:S(2)}) collective-permute-start(bf16[128,256]{1,0:T(8,128)(2,1)} %param.9), channel_id=1, source_target_pairs={{0,15},{1,0},{2,1},{3,2},{4,3},{5,4},{6,5},{7,6},{8,7},{9,8},{10,9... | collective-permute-start | bytes 196616 | tf_op jit(solution)/shard_map/ppermute | solution.py:29
  17.1 0.7 copy.22
  17.8 0.1 reduce-window.4
  17.9 0.1 reduce
  18.0 0.7 fusion.17
  18.7 0.9 select_reduce_fusion.4
  19.6 0.9 select_reduce_fusion
  20.5 4.3 %scatter_custom_fusion = s32[1984]{0:T(1024)S(1)} fusion(s32[1024]{0:T(1024)S(1)} %bitcast.28, s32[1024]{0:T(1024)S(1)} %iota.19, s32[]{:T(128)} %constant.133.clone.1), kind=kCustom, calls=%fused_computation.54 | custom fusion | bytes 7940 | tf_op jit(solution)/shard_map/scatter | solution.py:53
  24.9 4.3 %scatter_custom_fusion.1 = s32[1984]{0:T(1024)S(1)} fusion(s32[1024]{0:T(1024)S(1)} %bitcast.29, s32[1024]{0:T(1024)S(1)} %fusion.16, s32[]{:T(128)} %constant.134.clone.1), kind=kCustom, calls=%fused_computation.36 | custom fusion | bytes 7940 | tf_op jit(solution)/shard_map/scatter | solution.py:54
  29.3 0.1 broadcast_in_dim.66
  29.3 0.9 constant_dynamic-update-slice_fusion.15
  30.2 0.0 collective-permute-done
  30.2 1.9 collective-permute-start.2
  32.1 0.0 collective-permute-done.1
  32.1 6.7 %collective-permute-start.3 = (bf16[128,256]{1,0:T(8,128)(2,1)S(1)}, bf16[128,256]{1,0:T(8,128)(2,1)S(1)}, u32[]{:S(2)}, u32[]{:S(2)}) collective-permute-start(bf16[128,256]{1,0:T(8,128)(2,1)S(1)} %collective-permute-done.1), channel_id=1, source_target_pairs={{0,15},{1,0},{2,1},{3,2},{4,3},{5,4},{6,5},{7,6},{8,7},{9,8},{10,9... | collective-permute-start | bytes 196616 | tf_op jit(solution)/shard_map/ppermute | solution.py:29
  38.9 0.0 collective-permute-done.2
  38.9 1.9 collective-permute-start.4
  40.8 0.0 collective-permute-done.3
  40.8 6.7 %collective-permute-start.5 = (bf16[128,256]{1,0:T(8,128)(2,1)S(1)}, bf16[128,256]{1,0:T(8,128)(2,1)S(1)}, u32[]{:S(2)}, u32[]{:S(2)}) collective-permute-start(bf16[128,256]{1,0:T(8,128)(2,1)S(1)} %collective-permute-done.3), channel_id=1, source_target_pairs={{0,15},{1,0},{2,1},{3,2},{4,3},{5,4},{6,5},{7,6},{8,7},{9,8},{10,9... | collective-permute-start | bytes 196616 | tf_op jit(solution)/shard_map/ppermute | solution.py:29
  47.5 0.0 collective-permute-done.4
  47.6 1.9 collective-permute-start.6
  49.5 0.0 collective-permute-done.5
  49.5 6.7 %collective-permute-start.7 = (bf16[128,256]{1,0:T(8,128)(2,1)S(1)}, bf16[128,256]{1,0:T(8,128)(2,1)S(1)}, u32[]{:S(2)}, u32[]{:S(2)}) collective-permute-start(bf16[128,256]{1,0:T(8,128)(2,1)S(1)} %collective-permute-done.5), channel_id=1, source_target_pairs={{0,15},{1,0},{2,1},{3,2},{4,3},{5,4},{6,5},{7,6},{8,7},{9,8},{10,9... | collective-permute-start | bytes 196616 | tf_op jit(solution)/shard_map/ppermute | solution.py:29
  56.2 0.0 collective-permute-done.6
  56.2 1.9 collective-permute-start.8
  58.2 0.0 collective-permute-done.7
  58.2 6.7 %collective-permute-start.9 = (bf16[128,256]{1,0:T(8,128)(2,1)S(1)}, bf16[128,256]{1,0:T(8,128)(2,1)S(1)}, u32[]{:S(2)}, u32[]{:S(2)}) collective-permute-start(bf16[128,256]{1,0:T(8,128)(2,1)S(1)} %collective-permute-done.7), channel_id=1, source_target_pairs={{0,15},{1,0},{2,1},{3,2},{4,3},{5,4},{6,5},{7,6},{8,7},{9,8},{10,9... | collective-permute-start | bytes 196616 | tf_op jit(solution)/shard_map/ppermute | solution.py:29
  64.9 0.3 collective-permute-done.8
  65.2 1.9 collective-permute-start.10
  67.1 0.0 collective-permute-done.9
  67.1 7.0 %collective-permute-start.11 = (bf16[128,256]{1,0:T(8,128)(2,1)S(1)}, bf16[128,256]{1,0:T(8,128)(2,1)S(1)}, u32[]{:S(2)}, u32[]{:S(2)}) collective-permute-start(bf16[128,256]{1,0:T(8,128)(2,1)S(1)} %collective-permute-done.9), channel_id=1, source_target_pairs={{0,15},{1,0},{2,1},{3,2},{4,3},{5,4},{6,5},{7,6},{8,7},{9,8},{10,9... | collective-permute-start | bytes 196616 | tf_op jit(solution)/shard_map/ppermute | solution.py:29
  74.1 0.0 collective-permute-done.10
  74.1 1.9 collective-permute-start.12
  76.1 0.0 collective-permute-done.11
  76.1 6.7 %collective-permute-start.13 = (bf16[128,256]{1,0:T(8,128)(2,1)S(1)}, bf16[128,256]{1,0:T(8,128)(2,1)S(1)}, u32[]{:S(2)}, u32[]{:S(2)}) collective-permute-start(bf16[128,256]{1,0:T(8,128)(2,1)S(1)} %collective-permute-done.11), channel_id=1, source_target_pairs={{0,15},{1,0},{2,1},{3,2},{4,3},{5,4},{6,5},{7,6},{8,7},{9,8},{10,9... | collective-permute-start | bytes 196616 | tf_op jit(solution)/shard_map/ppermute | solution.py:29
  82.8 0.0 collective-permute-done.12
  82.8 1.9 collective-permute-start.14
  84.8 0.0 collective-permute-done.13
  84.8 6.4 %collective-permute-done.14 = bf16[128,256]{1,0:T(8,128)(2,1)S(1)} collective-permute-done((bf16[128,256]{1,0:T(8,128)(2,1)S(1)}, bf16[128,256]{1,0:T(8,128)(2,1)S(1)}, u32[]{:S(2)}, u32[]{:S(2)}) %collective-permute-start.14) | collective-permute-done | bytes 65568 | tf_op jit(solution)/shard_map/ppermute | solution.py:24
  91.2 0.0 copy-start.1
  91.2 0.0 copy-start
  91.2 4.5 %convolution_bitcast_fusion = f32[1024,256]{0,1:T(8,128)} fusion(bf16[2048,256]{1,0:T(8,128)(2,1)S(1)} %constant_dynamic-update-slice_fusion, bf16[2048,1024]{1,0:T(8,128)(2,1)} %param.8), kind=kOutput, calls=%fused_computation.5 | convolution fusion | flops 1073741824 | bytes 6291456 | tf_op jit(solution)/shard_map/dot_general | solution.py:82
  95.7 0.0 all-reduce.3.cloned.1.call-update
  95.7 0.1 dynamic-slice_convert_fusion
  95.8 0.1 broadcast_compare_fusion
  95.9 0.0 copy-done.1
  95.9 0.0 copy-done
  95.9 215.6 %all-reduce.3.cloned.1.call-done = f32[1024,256]{0,1:T(8,128)} async-done(((f32[1024,256]{0,1:T(8,128)}), f32[1024,256]{0,1:T(8,128)}) %all-reduce.3.cloned.1.call-update) | async-done | bytes 1048592 | tf_op jit(solution)/shard_map/psum | solution.py:88
  311.5 1.6 copy.23
  313.1 0.7 gather_fusion
  313.7 0.1 fusion.21
  313.8 0.1 copy.24
  313.9 0.7 gather_fusion.1
  314.6 0.1 copy.26
  314.7 0.7 gather_fusion.2
  315.3 0.1 copy.27
  315.5 1.1 fusion.1
  316.6 1.0 fusion.3
  (24 shorter events, 0.2 us)
Async XLA Ops:
  7.2 304.3 %all-reduce.3.cloned.1.call-start = ((), (), s32[]{:S(2)}) async-start(), calls=%async_computation | async-start | bytes 2097152 | tf_op jit(solution)/shard_map/psum | solution.py:88
  7.2 23.0 %collective-permute-start = (bf16[128,256]{1,0:T(8,128)(2,1)}, bf16[128,256]{1,0:T(8,128)(2,1)S(1)}, u32[]{:S(2)}, u32[]{:S(2)}) collective-permute-start(bf16[128,256]{1,0:T(8,128)(2,1)} %param.9), channel_id=1, source_target_pairs={{0,1},{1,2},{2,3},{3,4},{4,5},{5,6},{6,7},{7,8},{8,9},{9,10},{10,1... | collective-permute-start | bytes 196616 | tf_op jit(solution)/shard_map/ppermute | solution.py:24
  11.2 21.0 %collective-permute-start.1 = (bf16[128,256]{1,0:T(8,128)(2,1)}, bf16[128,256]{1,0:T(8,128)(2,1)S(1)}, u32[]{:S(2)}, u32[]{:S(2)}) collective-permute-start(bf16[128,256]{1,0:T(8,128)(2,1)} %param.9), channel_id=1, source_target_pairs={{0,15},{1,0},{2,1},{3,2},{4,3},{5,4},{6,5},{7,6},{8,7},{9,8},{10,9... | collective-permute-start | bytes 196616 | tf_op jit(solution)/shard_map/ppermute | solution.py:29
  30.2 8.7 %collective-permute-start.2 = (bf16[128,256]{1,0:T(8,128)(2,1)S(1)}, bf16[128,256]{1,0:T(8,128)(2,1)S(1)}, u32[]{:S(2)}, u32[]{:S(2)}) collective-permute-start(bf16[128,256]{1,0:T(8,128)(2,1)S(1)} %collective-permute-done), channel_id=1, source_target_pairs={{0,1},{1,2},{2,3},{3,4},{4,5},{5,6},{6,7},{7,8},{8,9},{9,10},{10,1... | collective-permute-start | bytes 196616 | tf_op jit(solution)/shard_map/ppermute | solution.py:24
  32.1 8.7 %collective-permute-start.3 = (bf16[128,256]{1,0:T(8,128)(2,1)S(1)}, bf16[128,256]{1,0:T(8,128)(2,1)S(1)}, u32[]{:S(2)}, u32[]{:S(2)}) collective-permute-start(bf16[128,256]{1,0:T(8,128)(2,1)S(1)} %collective-permute-done.1), channel_id=1, source_target_pairs={{0,15},{1,0},{2,1},{3,2},{4,3},{5,4},{6,5},{7,6},{8,7},{9,8},{10,9... | collective-permute-start | bytes 196616 | tf_op jit(solution)/shard_map/ppermute | solution.py:29
  38.9 8.7 %collective-permute-start.4 = (bf16[128,256]{1,0:T(8,128)(2,1)S(1)}, bf16[128,256]{1,0:T(8,128)(2,1)S(1)}, u32[]{:S(2)}, u32[]{:S(2)}) collective-permute-start(bf16[128,256]{1,0:T(8,128)(2,1)S(1)} %collective-permute-done.2), channel_id=1, source_target_pairs={{0,1},{1,2},{2,3},{3,4},{4,5},{5,6},{6,7},{7,8},{8,9},{9,10},{10,1... | collective-permute-start | bytes 196616 | tf_op jit(solution)/shard_map/ppermute | solution.py:24
  40.8 8.7 %collective-permute-start.5 = (bf16[128,256]{1,0:T(8,128)(2,1)S(1)}, bf16[128,256]{1,0:T(8,128)(2,1)S(1)}, u32[]{:S(2)}, u32[]{:S(2)}) collective-permute-start(bf16[128,256]{1,0:T(8,128)(2,1)S(1)} %collective-permute-done.3), channel_id=1, source_target_pairs={{0,15},{1,0},{2,1},{3,2},{4,3},{5,4},{6,5},{7,6},{8,7},{9,8},{10,9... | collective-permute-start | bytes 196616 | tf_op jit(solution)/shard_map/ppermute | solution.py:29
  47.6 8.7 %collective-permute-start.6 = (bf16[128,256]{1,0:T(8,128)(2,1)S(1)}, bf16[128,256]{1,0:T(8,128)(2,1)S(1)}, u32[]{:S(2)}, u32[]{:S(2)}) collective-permute-start(bf16[128,256]{1,0:T(8,128)(2,1)S(1)} %collective-permute-done.4), channel_id=1, source_target_pairs={{0,1},{1,2},{2,3},{3,4},{4,5},{5,6},{6,7},{7,8},{8,9},{9,10},{10,1... | collective-permute-start | bytes 196616 | tf_op jit(solution)/shard_map/ppermute | solution.py:24
  49.5 8.7 %collective-permute-start.7 = (bf16[128,256]{1,0:T(8,128)(2,1)S(1)}, bf16[128,256]{1,0:T(8,128)(2,1)S(1)}, u32[]{:S(2)}, u32[]{:S(2)}) collective-permute-start(bf16[128,256]{1,0:T(8,128)(2,1)S(1)} %collective-permute-done.5), channel_id=1, source_target_pairs={{0,15},{1,0},{2,1},{3,2},{4,3},{5,4},{6,5},{7,6},{8,7},{9,8},{10,9... | collective-permute-start | bytes 196616 | tf_op jit(solution)/shard_map/ppermute | solution.py:29
  56.2 8.9 %collective-permute-start.8 = (bf16[128,256]{1,0:T(8,128)(2,1)S(1)}, bf16[128,256]{1,0:T(8,128)(2,1)S(1)}, u32[]{:S(2)}, u32[]{:S(2)}) collective-permute-start(bf16[128,256]{1,0:T(8,128)(2,1)S(1)} %collective-permute-done.6), channel_id=1, source_target_pairs={{0,1},{1,2},{2,3},{3,4},{4,5},{5,6},{6,7},{7,8},{8,9},{9,10},{10,1... | collective-permute-start | bytes 196616 | tf_op jit(solution)/shard_map/ppermute | solution.py:24
  58.2 8.9 %collective-permute-start.9 = (bf16[128,256]{1,0:T(8,128)(2,1)S(1)}, bf16[128,256]{1,0:T(8,128)(2,1)S(1)}, u32[]{:S(2)}, u32[]{:S(2)}) collective-permute-start(bf16[128,256]{1,0:T(8,128)(2,1)S(1)} %collective-permute-done.7), channel_id=1, source_target_pairs={{0,15},{1,0},{2,1},{3,2},{4,3},{5,4},{6,5},{7,6},{8,7},{9,8},{10,9... | collective-permute-start | bytes 196616 | tf_op jit(solution)/shard_map/ppermute | solution.py:29
  65.2 8.9 %collective-permute-start.10 = (bf16[128,256]{1,0:T(8,128)(2,1)S(1)}, bf16[128,256]{1,0:T(8,128)(2,1)S(1)}, u32[]{:S(2)}, u32[]{:S(2)}) collective-permute-start(bf16[128,256]{1,0:T(8,128)(2,1)S(1)} %collective-permute-done.8), channel_id=1, source_target_pairs={{0,1},{1,2},{2,3},{3,4},{4,5},{5,6},{6,7},{7,8},{8,9},{9,10},{10,1... | collective-permute-start | bytes 196616 | tf_op jit(solution)/shard_map/ppermute | solution.py:24
  67.1 9.0 %collective-permute-start.11 = (bf16[128,256]{1,0:T(8,128)(2,1)S(1)}, bf16[128,256]{1,0:T(8,128)(2,1)S(1)}, u32[]{:S(2)}, u32[]{:S(2)}) collective-permute-start(bf16[128,256]{1,0:T(8,128)(2,1)S(1)} %collective-permute-done.9), channel_id=1, source_target_pairs={{0,15},{1,0},{2,1},{3,2},{4,3},{5,4},{6,5},{7,6},{8,7},{9,8},{10,9... | collective-permute-start | bytes 196616 | tf_op jit(solution)/shard_map/ppermute | solution.py:29
  74.1 8.7 %collective-permute-start.12 = (bf16[128,256]{1,0:T(8,128)(2,1)S(1)}, bf16[128,256]{1,0:T(8,128)(2,1)S(1)}, u32[]{:S(2)}, u32[]{:S(2)}) collective-permute-start(bf16[128,256]{1,0:T(8,128)(2,1)S(1)} %collective-permute-done.10), channel_id=1, source_target_pairs={{0,1},{1,2},{2,3},{3,4},{4,5},{5,6},{6,7},{7,8},{8,9},{9,10},{10,1... | collective-permute-start | bytes 196616 | tf_op jit(solution)/shard_map/ppermute | solution.py:24
  76.1 8.7 %collective-permute-start.13 = (bf16[128,256]{1,0:T(8,128)(2,1)S(1)}, bf16[128,256]{1,0:T(8,128)(2,1)S(1)}, u32[]{:S(2)}, u32[]{:S(2)}) collective-permute-start(bf16[128,256]{1,0:T(8,128)(2,1)S(1)} %collective-permute-done.11), channel_id=1, source_target_pairs={{0,15},{1,0},{2,1},{3,2},{4,3},{5,4},{6,5},{7,6},{8,7},{9,8},{10,9... | collective-permute-start | bytes 196616 | tf_op jit(solution)/shard_map/ppermute | solution.py:29
  82.8 8.3 %collective-permute-start.14 = (bf16[128,256]{1,0:T(8,128)(2,1)S(1)}, bf16[128,256]{1,0:T(8,128)(2,1)S(1)}, u32[]{:S(2)}, u32[]{:S(2)}) collective-permute-start(bf16[128,256]{1,0:T(8,128)(2,1)S(1)} %collective-permute-done.12), channel_id=1, source_target_pairs={{0,1},{1,2},{2,3},{3,4},{4,5},{5,6},{6,7},{7,8},{8,9},{9,10},{10,1... | collective-permute-start | bytes 196616 | tf_op jit(solution)/shard_map/ppermute | solution.py:24
  91.2 4.7 %copy-start.1 = (s32[136]{0:T(256)S(1)}, s32[136]{0:T(256)}, u32[]{:S(2)}) copy-start(s32[136]{0:T(256)} %constant.173) | copy-start | bytes 1636
  91.2 4.7 %copy-start = (s32[136]{0:T(256)S(1)}, s32[136]{0:T(256)}, u32[]{:S(2)}) copy-start(s32[136]{0:T(256)} %constant.174) | copy-start | bytes 1636
Sparse Core Ops, SparseCore 0:
  95.8 215.6 all-reduce.2
